TPU v7x, 128 devices: a whole 4x4x4 slice. The times are simulated.
128 devices in a mesh: stn: 16 (over x, y_lo, core), tm: 8 (over z, y_hi).
Axes of the slice: x: 4, y: 4 (y_hi: 2, y_lo: 2; y = y_hi * 2 + y_lo), z: 4, core: 2. Of those that a mesh axis runs over, the one named last changes fastest.
Arguments:
- samples: bfloat16 [1024, 1048576], P('stn', 'tm'), may hold values from -6 to 6
Outputs:
- visibilities: float32 [128, 2, 1024, 1024], P(('stn', 'tm'))
All inputs are finite; a program needn't handle non-finite values.
Results may differ from a plain program's by a relative error of at most 0.0062.
Values may be sent and summed in bfloat16 or wider, within the bound.
A program may use at most 256 MiB of HBM per device.

v0:
```python
import jax
import jax.numpy as jnp
from jax import lax
from jax.sharding import PartitionSpec as P

FRAME = 8192
TAPS = 12
CH_DEV = 1


def passed_along(array, axis, by):
    peers = lax.axis_size(axis)
    pairs = [(i, i + by) for i in range(peers) if 0 <= i + by < peers]
    return lax.ppermute(array, axis, pairs)


def prototype():
    length = TAPS * FRAME
    place = jnp.arange(length, dtype=jnp.int32).astype(jnp.float32)
    centred = (place - 0.5 * length + 0.5) / FRAME
    window = 0.54 - 0.46 * jnp.cos(2.0 * jnp.pi * place / (length - 1))
    return (jnp.sinc(centred) * window).reshape(TAPS, FRAME)


def transform_table(kept_channels, first_channel):
    sample_index = jnp.arange(FRAME, dtype=jnp.int32)
    column = jnp.arange(2 * kept_channels, dtype=jnp.int32)
    channel = first_channel + column // 2
    phase = channel[:, None] * sample_index[None, :] % FRAME
    angle = 2.0 * jnp.pi / FRAME * phase.astype(jnp.float32)
    scaling = (2.0 / FRAME) ** 0.5
    table = jnp.where((column % 2 == 0)[:, None], jnp.cos(angle), -jnp.sin(angle)) * scaling
    return table.astype(jnp.bfloat16)


def filter_frames(padded, prototype_taps, out_frames):
    margin_frames = TAPS - 1
    frame_major = jnp.swapaxes(padded, 0, 1)
    running = jnp.zeros((out_frames, padded.shape[0], FRAME), jnp.float32)
    for tap_index in range(TAPS):
        begin = margin_frames - tap_index
        running = running + prototype_taps[tap_index] * frame_major[
            begin : begin + out_frames
        ].astype(jnp.float32)
    return running


def project_spectra(transform, filtered):
    return lax.dot_general(
        transform, filtered, (((1,), (2,)), ((), ())), preferred_element_type=jnp.float32
    )


def on_device(samples):
    station_inputs, sample_count = samples.shape
    frame_count = sample_count // FRAME
    margin_frames = TAPS - 1
    stations = lax.axis_size("stn")
    time_blocks = lax.axis_size("tm")
    kept_channels = CH_DEV * stations * time_blocks
    first_channel = FRAME // 4 - kept_channels // 2
    prototype_taps = prototype()
    transform = transform_table(kept_channels, first_channel)
    blocks = samples.reshape(station_inputs, frame_count, FRAME)
    zero_frames = jnp.zeros((station_inputs, margin_frames, FRAME), samples.dtype)
    tail_padded = jnp.concatenate([blocks[:, frame_count - margin_frames :], zero_frames], axis=1)
    carried = filter_frames(tail_padded, prototype_taps, margin_frames)
    arrived = passed_along(carried, "tm", 1)
    padded = jnp.concatenate([zero_frames, blocks], axis=1)
    running = filter_frames(padded, prototype_taps, frame_count)
    running = jnp.concatenate([running[:margin_frames] + arrived, running[margin_frames:]], axis=0)
    combined = project_spectra(transform, running.astype(jnp.bfloat16))
    rounded = combined.astype(jnp.bfloat16).reshape(2 * kept_channels, frame_count * station_inputs)
    turned = lax.all_to_all(
        rounded.reshape(2 * kept_channels, 1, frame_count * station_inputs),
        ("stn", "tm"),
        split_axis=0,
        concat_axis=1,
        tiled=True,
    )
    arranged = turned.reshape(CH_DEV, 2, stations, time_blocks, frame_count, station_inputs)
    swapped = jnp.stack([arranged[:, 1], -arranged[:, 0]], axis=1)
    real_part = jnp.einsum(
        "crstfi,crutfj->csiuj", arranged, arranged, preferred_element_type=jnp.float32
    )
    imag_part = jnp.einsum(
        "crstfi,crutfj->csiuj", swapped, arranged, preferred_element_type=jnp.float32
    )
    all_inputs = stations * station_inputs
    real_part = real_part.reshape(CH_DEV, all_inputs, all_inputs)
    imag_part = imag_part.reshape(CH_DEV, all_inputs, all_inputs)
    return jnp.stack([real_part, imag_part], axis=1) * (1.0 / (time_blocks * frame_count))


def solution(mesh):
    placed = (P("stn", "tm"),)
    return jax.shard_map(
        on_device,
        mesh=mesh,
        in_specs=placed,
        out_specs=P(("stn", "tm"), None, None, None),
        check_vma=False,
    )
```

profile of v0, /device:TPU:1, one launch (start us, length us, event | category | flops | bytes accessed | tf_op | source)
XLA Modules:
  0.0 653.1 jit_solution(3653302438730252341)
XLA Ops:
  0.0 1.8 fusion.29
  1.8 8.6 %copy.21 = bf16[8,16,8,8192]{3,2,0,1:T(8,128)(2,1)S(1)} copy(bf16[8,16,8,8192]{3,2,1,0:T(8,128)(2,1)} %bitcast.59) | data formatting | bytes 33554432 | tf_op jit(solution)/shard_map/reshape | solution.py:64
  10.4 0.0 copy-start
  10.4 1.8 slice.238
  12.2 12.6 %pad_bitcast_fusion.1 = bf16[22,64,8192]{2,1,0:T(8,128)(2,1)} fusion(bf16[64,11,8192]{2,0,1:T(8,128)(2,1)S(1)} %slice.238), kind=kLoop, calls=%fused_computation.5 | loop fusion | bytes 34603008 | tf_op jit(solution)/shard_map/transpose | solution.py:38
  24.8 0.0 copy-done
  24.8 57.3 %multiply_add_fusion.1 = f32[11,64,8192]{2,1,0:T(8,128)} fusion(bf16[22,64,8192]{2,1,0:T(8,128)(2,1)} %pad_bitcast_fusion.1, f32[8192]{0:T(1024)S(1)} %get-tuple-element.8, f32[8192]{0:T(1024)S(1)} %get-tuple-element.9, f32[8192]{0:T(1024)S(1)} %get-tuple-element.10, f32[8192]{0:T(1024)S(1)} %get-tuple-element.11, f32[8192]{0:T(1024)S(1)} %get-tuple-element.12, ...), kind=kLoop, calls=%fused_computation.4 | loop fusion | flops 201850880 | bytes 161873920 | tf_op jit(solution)/shard_map/add | solution.py:42
  82.1 13.2 %collective-permute-start = (f32[11,64,8192]{2,1,0:T(8,128)}, f32[11,64,8192]{2,1,0:T(8,128)}, u32[]{:S(2)}, u32[]{:S(2)}) collective-permute-start(f32[11,64,8192]{2,1,0:T(8,128)} %multiply_add_fusion.1), channel_id=1, source_target_pairs={{0,1},{1,2},{2,3},{3,4},{4,5},{5,6},{6,7},{8,9},{9,10},{10,11},{11... | collective-permute-start | bytes 69206024 | tf_op jit(solution)/shard_map/ppermute | solution.py:14
  95.4 15.8 %pad_bitcast_fusion = bf16[27,64,8192]{2,1,0:T(8,128)(2,1)} fusion(bf16[64,16,8192]{2,0,1:T(8,128)(2,1)} %bitcast.58), kind=kLoop, calls=%fused_computation.1 | loop fusion | bytes 45088768 | tf_op jit(solution)/shard_map/transpose | solution.py:38
  111.1 79.4 %multiply_add_fusion = f32[16,64,8192]{2,1,0:T(8,128)} fusion(bf16[27,64,8192]{2,1,0:T(8,128)(2,1)} %pad_bitcast_fusion, f32[8192]{0:T(1024)S(1)} %get-tuple-element.8, f32[8192]{0:T(1024)S(1)} %get-tuple-element.9, f32[8192]{0:T(1024)S(1)} %get-tuple-element.10, f32[8192]{0:T(1024)S(1)} %get-tuple-element.11, f32[8192]{0:T(1024)S(1)} %get-tuple-element.12, ...), kind=kLoop, calls=%fused_computation | loop fusion | flops 293601280 | bytes 235274240 | tf_op jit(solution)/shard_map/add | solution.py:42
  190.6 7.1 %slice.283 = bf16[5,64,8192]{2,1,0:T(8,128)(2,1)} slice(f32[16,64,8192]{2,1,0:T(8,128)} %multiply_add_fusion), slice={[11:16], [0:64], [0:8192]} | slice | bytes 10485760 | tf_op jit(solution)/shard_map/slice | solution.py:71
  197.7 35.9 %fusion.59 = bf16[256,8192,1]{1,0,2:T(8,128)(2,1)} fusion(s32[256]{0:T(256)S(1)} %fusion.38, pred[256]{0:T(512)(128)(4,1)S(1)} %fusion.40), kind=kLoop, calls=%fused_computation.23.clone.clone.clone.clone.2 | loop fusion | flops 37748736 | bytes 4195584 | tf_op jit(solution)/shard_map/dot_general | solution.py:49
  233.6 348.2 %collective-permute-done = f32[11,64,8192]{2,1,0:T(8,128)} collective-permute-done((f32[11,64,8192]{2,1,0:T(8,128)}, f32[11,64,8192]{2,1,0:T(8,128)}, u32[]{:S(2)}, u32[]{:S(2)}) %collective-permute-start) | collective-permute-done | bytes 23068704 | tf_op jit(solution)/shard_map/ppermute | solution.py:14
  581.8 19.6 %fusion = bf16[11,64,8192]{2,1,0:T(8,128)(2,1)} fusion(f32[11,64,8192]{2,1,0:T(8,128)} %collective-permute-done, f32[16,64,8192]{2,1,0:T(8,128)} %multiply_add_fusion), kind=kLoop, calls=%fused_computation.3 | loop fusion | flops 11534336 | bytes 57671680 | tf_op jit(solution)/shard_map/convert
  601.4 9.5 %fusion.20 = bf16[256,16,64]{0,2,1:T(8,128)(2,1)S(1)} fusion(bf16[5,64,8192]{2,1,0:T(8,128)(2,1)} %slice.283, bf16[11,64,8192]{2,1,0:T(8,128)(2,1)} %fusion, bf16[256,8192,1]{1,0,2:T(8,128)(2,1)} %fusion.59), kind=kOutput, calls=%fused_computation.33 | convolution fusion | flops 4328783872 | bytes 21495808 | tf_op jit(solution)/shard_map/dot_general | solution.py:49
  610.9 0.5 broadcast.107
  611.4 1.0 reduce.1
  612.4 0.2 copy.23
  612.6 0.2 reshape.146
  612.8 26.1 %all_to_all.15 = bf16[128,2,1024]{2,1,0:T(2,128)(2,1)S(1)} all-to-all(bf16[128,2,1024]{2,1,0:T(2,128)(2,1)S(1)} %reshape.146), channel_id=1, replica_groups=mesh['stn'=16,'tm'=8] {'stn','tm'}, dimensions={0} | all-to-all | bytes 1048576 | tf_op jit(solution)/shard_map/all_to_all | solution.py:74
  639.0 0.4 reshape.147
  639.4 3.1 reduce
  642.5 0.2 all_to_all.12
  642.7 0.1 copy.12
  642.8 0.7 reshape.139
  643.4 0.7 reshape.137
  644.1 0.1 fusion.47
  644.2 0.2 maximum_bitcast_fusion
  644.5 0.7 copy.15
  645.1 0.7 reshape.141
  645.9 0.7 copy.13
  646.6 0.7 reshape.138
  647.3 0.7 convolution_bitcast_fusion.1
  648.0 0.7 convolution_bitcast_fusion
  648.8 4.4 maximum_multiply_fusion
  (3 shorter events, 0.0 us)
Async XLA Ops:
  10.4 14.4 %copy-start = (bf16[8,16,8,8192]{3,2,0,1:T(8,128)(2,1)}, bf16[8,16,8,8192]{3,2,0,1:T(8,128)(2,1)S(1)}, u32[]{:S(2)}) copy-start(bf16[8,16,8,8192]{3,2,0,1:T(8,128)(2,1)S(1)} %copy.21) | copy-start | bytes 50331652
  82.1 499.7 %collective-permute-start = (f32[11,64,8192]{2,1,0:T(8,128)}, f32[11,64,8192]{2,1,0:T(8,128)}, u32[]{:S(2)}, u32[]{:S(2)}) collective-permute-start(f32[11,64,8192]{2,1,0:T(8,128)} %multiply_add_fusion.1), channel_id=1, source_target_pairs={{0,1},{1,2},{2,3},{3,4},{4,5},{5,6},{6,7},{8,9},{9,10},{10,11},{11... | collective-permute-start | bytes 69206024 | tf_op jit(solution)/shard_map/ppermute | solution.py:14
where the time goes:
time: 653 us
  waiting for transfers between devices  348 us (53%)
  other arithmetic  203 us (31%)
  local copies, waits for them, and re-layouts  51.6 us (8%)
  blocking collectives  26.1 us (4%)
  starting transfers between devices  13.2 us (2%)
  matrix products  10.9 us (2%)
    ppermute x1, waiting for transfers between devices, passed_along(): return lax.ppermute(array, axis, pairs)  348 us
    add x2, other arithmetic, filter_frames(): running + prototype_taps[tap_index] * frame_major[begin:begin + out_frame...  137 us
    dot_general x1, other arithmetic, project_spectra(): lax.dot_general(transform, filtered, (((1,), (2,)), ((), ())), preferred_...  35.9 us
    transpose x2, local copies, waits for them, and re-layouts, filter_frames(): frame_major = jnp.swapaxes(padded, 0, 1)  28.3 us
    all_to_all x1, blocking collectives, on_device(): lax.all_to_all(rounded.reshape(2 * kept_channels, 1, frame_count * statio...  26.1 us
    another operation x1, other arithmetic  19.6 us
    ppermute x1, starting transfers between devices, passed_along(): return lax.ppermute(array, axis, pairs)  13.2 us
  transfers between devices with their start and end apart: 1, of which 1 were waited for; matrix products, arithmetic and copies ran while one was open for 21% of the time, Pallas kernels for 0%

commit v1 on v0

v1 whole, which is shorter than its diff:
```python
import functools
import numpy as np
import jax
import jax.numpy as jnp
from jax import lax
from jax.experimental import pallas as pl
from jax.experimental.pallas import tpu as pltpu

FRAME = 8192
TAPS = 12
GROUP = 16
OUT = 27
BLK = 1024
QUARTER = FRAME // 4
KEPT = 128
bf = jnp.bfloat16
f32 = jnp.float32


def prototype():
    length = TAPS * FRAME
    place = np.arange(length, dtype=np.float32)
    centred = (place - np.float32(0.5 * length - 0.5)) / np.float32(FRAME)
    window = np.float32(0.54) - np.float32(0.46) * np.cos(2.0 * np.pi * place.astype(np.float64) / (length - 1)).astype(np.float32)
    return (np.sinc(centred.astype(np.float64)).astype(np.float32) * window).reshape(TAPS, FRAME)


def table():
    n = np.arange(QUARTER)
    col = np.arange(128)
    chan = (col % 32) * 4 + col // 32
    phase = (n[:, None] * (chan[None, :] + 1984)) % FRAME
    ang = (np.float32(2.0 * np.pi / FRAME) * phase.astype(np.float32)).astype(np.float64)
    sc = np.float32((2.0 / FRAME) ** 0.5)
    re = np.cos(ang).astype(np.float32) * sc
    im = -np.sin(ang).astype(np.float32) * sc
    return np.concatenate([re, im], axis=1)


ORDER = [0, 11, 1, 10, 2, 9, 3, 8, 4, 7, 5, 6]


def rot(d, q, r, p):
    k = (q * r) % 4
    return [((1, 0), (1, 1)), ((1, 1), (-1, 0)), ((-1, 0), (-1, 1)), ((-1, 1), (1, 0))][k][p]


def kernel_a(*refs, frames):
    x_refs = refs[:frames]
    h_ref, t_ref, out_ref, hrep, filt, acc, slab = refs[frames:]
    out_frames = frames + TAPS - 1
    g = pl.program_id(0)
    i = pl.program_id(1)
    n0 = pl.multiple_of(i * BLK, BLK)

    @pl.when(g == 0)
    def _():
        for k in range(TAPS):
            row = h_ref[k:k + 1, pl.ds(n0, BLK)]
            hrep[k * 8:(k + 1) * 8, pl.ds(n0, BLK)] = jnp.broadcast_to(row, (8, BLK)).astype(bf)

    @pl.when(i == 0)
    def _():
        acc[...] = jnp.zeros_like(acc)

    for j in range(BLK // 256):
        lanes = slice(j * 256, (j + 1) * 256)
        hl = pl.ds(pl.multiple_of(n0 + j * 256, 256), 256)
        hs = [hrep[k * 8:(k + 1) * 8, hl] for k in range(TAPS)]
        for half in range(2):
            rows = slice(half * 8, half * 8 + 8)
            xs = [x[rows, lanes] for x in x_refs]
            for t in range(out_frames):
                s = None
                for k in ORDER:
                    if 0 <= t - k < frames:
                        p = hs[k] * xs[t - k]
                        s = p if s is None else s + p
                filt[t * 16 + half * 8:t * 16 + half * 8 + 8, lanes] = s

    tq = pl.multiple_of((i % (QUARTER // BLK)) * BLK, BLK)
    d = jnp.dot(filt[...], t_ref[pl.ds(tq, BLK), :], preferred_element_type=f32)
    q = i // (QUARTER // BLK)
    for qq in range(4):
        @pl.when(q == qq)
        def _():
            if qq == 0:
                acc[...] += d
            else:
                lane = lax.broadcasted_iota(jnp.int32, (1, 128), 1)
                r = lane // 32
                dre, dim = d[:, :128], d[:, 128:]
                for p in range(2):
                    v = None
                    for rr in range(4):
                        sg, src = rot(None, qq, rr, p)
                        w = (dre, dim)[src]
                        w = w if sg > 0 else -w
                        v = w if v is None else jnp.where(r == rr, w, v)
                    acc[:, p * 128:(p + 1) * 128] += v

    @pl.when(i == pl.num_programs(1) - 1)
    def _():
        for b in range(4):
            lo, hi = b * 128, min((b + 1) * 128, out_frames * 16)
            for p in range(2):
                blk = acc[lo:hi, p * 128:(p + 1) * 128]
                if hi - lo < 128:
                    blk = jnp.concatenate([blk, jnp.zeros((128 - (hi - lo), 128), f32)], axis=0)
                tr = blk.T
                row = (b // 2) * 4 + p * 2 + b % 2
                for r in range(4):
                    slab[pl.ds(r * 8 + row, 32, stride=32), :] = tr[r * 32:(r + 1) * 32]
        out_ref[...] = slab[...].astype(bf)


def run_a(x):
    inputs, samples = x.shape
    frames = samples // FRAME
    steps = FRAME // BLK
    groups = inputs // GROUP
    out_frames = frames + TAPS - 1
    h = jnp.asarray(prototype())
    t = jnp.asarray(table()).astype(bf)
    specs = [pl.BlockSpec((GROUP, BLK), functools.partial(lambda f, g, i: (g, f * steps + i), f)) for f in range(frames)]
    return pl.pallas_call(
        functools.partial(kernel_a, frames=frames),
        grid=(groups, steps),
        in_specs=specs + [pl.BlockSpec(h.shape, lambda g, i: (0, 0)), pl.BlockSpec(t.shape, lambda g, i: (0, 0))],
        out_specs=pl.BlockSpec((None, KEPT * 8, 128), lambda g, i: (g, 0, 0)),
        out_shape=jax.ShapeDtypeStruct((groups, KEPT * 8, 128), bf),
        scratch_shapes=[
            pltpu.VMEM((TAPS * 8, FRAME), bf),
            pltpu.VMEM((out_frames * 16, BLK), bf),
            pltpu.VMEM((out_frames * 16, 256), f32),
            pltpu.VMEM((KEPT * 8, 128), f32),
        ],
        compiler_params=pltpu.CompilerParams(dimension_semantics=("arbitrary", "arbitrary"), vmem_limit_bytes=60 * 2**20),
    )(*([x] * frames), h, t)


def kernel_c(r_ref, out_ref, gmat, gswap, *, stations, blocks, groups):
    depth = 2 * blocks * 16
    scale = 1.0 / (blocks * 16)

    @pl.when(pl.program_id(0) == 0)
    def _():
        row = lax.broadcasted_iota(jnp.int32, (8, 128), 0)
        lane = lax.broadcasted_iota(jnp.int32, (8, 128), 1)

        def station_pair(sp, carry):
            pieces = []
            for sg in range(8):
                s = sp * 2 + sg // 4
                g = sg % 4
                v = [r_ref[g, pl.ds(pl.multiple_of((s * blocks + m) * 8, 8), 8), :].astype(f32) for m in range(blocks)]
                rolled = [pltpu.roll(x, 4, 0) for x in v]
                rows = []
                for m in range(0, blocks, 2):
                    lo = rolled[m - 1] if m > 0 else jnp.zeros_like(v[0])
                    rows.append(v[m] + jnp.where(row < 4, lo, rolled[m + 1]))
                pieces.append(rows)
            for j in range(blocks // 2):
                a = [pieces[sg][j] for sg in range(8)]
                for d in (4, 2, 1):
                    low = (lane // 16) // d % 2 == 0
                    new = list(a)
                    for i in range(8):
                        if i // d % 2 == 0:
                            new[i] = jnp.where(low, a[i], pltpu.roll(a[i + d], 16 * d, 1))
                            new[i + d] = jnp.where(low, pltpu.roll(a[i], 128 - 16 * d, 1), a[i + d])
                    a = new
                cols = pl.ds(pl.multiple_of(sp * 128, 128), 128)
                for t8 in range(8):
                    x = a[t8]
                    k0 = t8 * (blocks * 4) + j * 8
                    gmat[k0:k0 + 8, cols] = x.astype(bf)
                    sw = jnp.where(row % 4 < 2, pltpu.roll(x, 6, 0), -pltpu.roll(x, 2, 0))
                    gswap[k0:k0 + 8, cols] = sw.astype(bf)
            return carry

        lax.fori_loop(0, stations // 2, station_pair, 0)

    rows_out = out_ref.shape[1]
    cols = pl.ds(pl.multiple_of(pl.program_id(0) * rows_out, rows_out), rows_out)
    g = gmat[...]
    dims = (((0,), (0,)), ((), ()))
    out_ref[0] = lax.dot_general(gmat[:, cols], g, dims, preferred_element_type=f32) * scale
    out_ref[1] = lax.dot_general(gswap[:, cols], g, dims, preferred_element_type=f32) * scale


def run_c(r, stations=16, blocks=8):
    groups = r.shape[0]
    inputs = stations * groups * GROUP
    depth = 2 * blocks * 16
    tile = 128
    return pl.pallas_call(
        functools.partial(kernel_c, stations=stations, blocks=blocks, groups=groups),
        grid=(inputs // tile,),
        in_specs=[pl.BlockSpec(r.shape, lambda i: (0, 0, 0))],
        out_specs=pl.BlockSpec((None, 2, tile, inputs), lambda i: (0, 0, i, 0)),
        out_shape=jax.ShapeDtypeStruct((1, 2, inputs, inputs), f32),
        scratch_shapes=[pltpu.VMEM((depth, inputs), bf), pltpu.VMEM((depth, inputs), bf)],
        compiler_params=pltpu.CompilerParams(dimension_semantics=("arbitrary",), vmem_limit_bytes=40 * 2**20),
    )(r)


def on_device(samples):
    stations = lax.axis_size("stn")
    blocks = lax.axis_size("tm")
    sent = run_a(samples)
    groups = sent.shape[0]
    devices = stations * blocks
    got = lax.all_to_all(
        sent.reshape(groups, devices, 8, 128), ("stn", "tm"), split_axis=1, concat_axis=1, tiled=True
    )
    return run_c(got.reshape(groups, devices * 8, 128), stations, blocks)


def solution(mesh):
    return jax.shard_map(
        on_device,
        mesh=mesh,
        in_specs=(jax.sharding.PartitionSpec("stn", "tm"),),
        out_specs=jax.sharding.PartitionSpec(("stn", "tm"), None, None, None),
        check_vma=False,
    )
```

time: 653 us -> 77.9 us (0.12)
  waiting for transfers between devices: 348 us -> 0 us
  other arithmetic: 203 us -> 0 us
  local copies, waits for them, and re-layouts: 51.6 us -> 1.59 us
  Pallas kernels: 0 us -> 45.4 us
  starting transfers between devices: 13.2 us -> 0 us
  matrix products: 10.9 us -> 0 us
    ppermute x1 -> x0, waiting for transfers between devices: 348 us -> none  [passed_along(): return lax.ppermute(array, axis, pairs)]
    add x3 -> x0, other arithmetic: 137 us -> none  [the longest x2 137 us: filter_frames(): running + prototype_taps[tap_index] * frame_major[begin:begin + out_frame...]
    pallas_call x0 -> x2, Pallas kernels: none -> 45.4 us  [the longest x1 37.5 us: run_a(): pl.pallas_call(functools.partial(kernel_a, frames=frames), grid=(groups,...]
    dot_general x2 -> x0, other arithmetic: 36.1 us -> none  [the longest x1 35.9 us: project_spectra(): lax.dot_general(transform, filtered, (((1,), (2,)), ((), ())), preferred_...]
    transpose x2 -> x0, local copies, waits for them, and re-layouts: 28.3 us -> none  [filter_frames(): frame_major = jnp.swapaxes(padded, 0, 1)]
    another operation x2 -> x0, other arithmetic: 20.6 us -> none
    ppermute x1 -> x0, starting transfers between devices: 13.2 us -> none  [passed_along(): return lax.ppermute(array, axis, pairs)]
    dot_general x3 -> x0, matrix products: 10.9 us -> none  [the longest x1 9.47 us: project_spectra(): lax.dot_general(transform, filtered, (((1,), (2,)), ((), ())), preferred_...]
  transfers between devices with their start and end apart: 1 -> 0, of which waited for: 1 -> 0; matrix products, arithmetic and copies ran while one was open for 21% -> 0% of each run, Pallas kernels for 0% -> 0%
where the time goes in v1:
time: 77.9 us; the launch traced here: 77.7 us
  Pallas kernels  45.4 us (58%)
  blocking collectives  30.8 us (40%)
  local copies, waits for them, and re-layouts  1.59 us (2%)
    pallas_call x1, Pallas kernels, run_a(): pl.pallas_call(functools.partial(kernel_a, frames=frames), grid=(groups,...  37.5 us
    all_to_all x1, blocking collectives, on_device(): lax.all_to_all(sent.reshape(groups, devices, 8, 128), ('stn', 'tm'), spli...  30.8 us
    pallas_call x1, Pallas kernels, run_c(): pl.pallas_call(functools.partial(kernel_c, stations=stations, blocks=bloc...  7.9 us

profile of v1, /device:TPU:1, one launch (start us, length us, event | category | flops | bytes accessed | tf_op | source)
XLA Modules:
  0.0 77.7 jit_solution(917947939724967230)
XLA Ops:
  0.0 37.5 %shard_map.37 = bf16[4,1024,128]{2,1,0:T(8,128)(2,1)} custom-call(bf16[64,131072]{1,0:T(8,128)(2,1)} %refs_15_.1, bf16[64,131072]{1,0:T(8,128)(2,1)} %refs_15_.1, bf16[64,131072]{1,0:T(8,128)(2,1)} %refs_15_.1, bf16[64,131072]{1,0:T(8,128)(2,1)} %refs_15_.1, bf16[64,131072]{1,0:T(8,128)(2,1)} %refs_15_.1, bf16[64,131072]{1,0:T(8,128)(2,1)} %refs_15_.1, ...), custom_call_target="tpu_custom_call" | custom-call | tf_op jit(solution)/shard_map/pallas_call | solution.py:126
  37.5 1.4 %copy.4 = bf16[4,128,8,128]{3,2,0,1:T(8,128)(2,1)S(1)} copy(bf16[4,128,8,128]{3,2,1,0:T(8,128)(2,1)} %bitcast.5) | data formatting | bytes 2097152 | tf_op jit(solution)/shard_map/reshape | solution.py:215
  38.9 30.8 %all_to_all.5 = bf16[4,128,8,128]{3,2,0,1:T(8,128)(2,1)S(1)} all-to-all(bf16[4,128,8,128]{3,2,0,1:T(8,128)(2,1)S(1)} %copy.4), channel_id=1, replica_groups=mesh['stn'=16,'tm'=8] {'stn','tm'}, dimensions={1} | all-to-all | bytes 2097152 | tf_op jit(solution)/shard_map/all_to_all | solution.py:214
  69.7 0.2 copy.7
  69.8 7.9 %shard_map.38 = f32[1,2,1024,1024]{3,2,1,0:T(8,128)} custom-call(bf16[4,1024,128]{2,1,0:T(8,128)(2,1)S(1)} %bitcast.4), custom_call_target="tpu_custom_call" | custom-call | tf_op jit(solution)/shard_map/pallas_call | solution.py:197
